TPU v7x, 256 devices: a whole 4x4x8 slice. The times are simulated.
256 devices in a mesh: freq: 8 (over z), lat: 8 (over x, y_hi), lon: 4 (over y_lo, core).
Axes of the slice: x: 4, y: 4 (y_hi: 2, y_lo: 2; y = y_hi * 2 + y_lo), z: 8, core: 2. Of those that a mesh axis runs over, the one named last changes fastest.
Arguments:
- direction: float32 [3, 32, 1024, 2048], P(None, 'freq', 'lat', 'lon'), may hold values from -6 to 6
- base_flow: float32 [2, 32, 1024, 2048], P(None, 'freq', 'lat', 'lon'), may hold values from -2 to 2
- water_depth: float32 [1024, 2048], P('lat', 'lon'), may hold values from 0.5 to 2
- drag_factor: float32 [1024, 2048], P('lat', 'lon'), may hold values from 0.2 to 2
- wet_mask: int32 [1024, 2048], P('lat', 'lon'), may hold values 0 or 1
Outputs:
- result: float32 [3, 32, 1024, 2048], P(None, 'freq', 'lat', 'lon')
All inputs are finite; a program needn't handle non-finite values. No bound on the sum of `wet_mask` on one device may be relied on, other than what follows from the above.
Results may differ from a plain program's by a relative error of at most 0.000071.
Values sent between devices are 32-bit elements; how exact they have to be, the bound alone decides.
A program may use at most 128 MiB of HBM per device.

v0:
```python
import math
import jax
import jax.numpy as jnp
from jax import lax
from jax.sharding import PartitionSpec as P

NCON = 16
NTIME = 256
LINEAR_DRAG = 0.5
GRAVITY = 1.0
OMEGA_STEP = 0.25
SPEED_SOFT = 0.01


def extended_2(block, sides, width):
    for axis, dim in sides:
        count = lax.axis_size(axis)
        forward = [(i, i + 1) for i in range(count - 1)]
        forward.append((count - 1, 0))
        backward = [(target, source) for source, target in forward]
        low = lax.ppermute(
            lax.slice_in_dim(block, block.shape[dim] - width, None, axis=dim), axis, forward
        )
        high = lax.ppermute(lax.slice_in_dim(block, 0, width, axis=dim), axis, backward)
        block = jnp.concatenate([low, block, high], axis=dim)
    return block


def samples_table(sample_count, constituents):
    sample_index = jnp.arange(sample_count, dtype=jnp.int32)
    harmonic = jnp.arange(1, constituents + 1, dtype=jnp.int32)
    wrapped_turns = sample_index[:, None] * harmonic[None, :] % sample_count
    phase_angle = wrapped_turns.astype(jnp.float32) * (2.0 * math.pi / sample_count)
    table = jnp.stack([jnp.cos(phase_angle), jnp.sin(phase_angle)], axis=2)
    return table.reshape(sample_count, 2 * constituents)


def rotation_of(row_index, total_rows):
    return 0.5 + (row_index.astype(jnp.float32) + 0.5) / total_rows


def tendency(values, angular):
    cos_sin = values.reshape((values.shape[0] // 2, 2) + values.shape[1:])
    moved = jnp.stack([angular * cos_sin[:, 1], -angular * cos_sin[:, 0]], axis=1)
    return moved.reshape(values.shape)


def linear_residual(extended, tile_rows, tile_cols, angular, rotation):

    def neighbour(plane, row_step, col_step):
        return extended[
            plane,
            :,
            1 + row_step : 1 + row_step + tile_rows,
            1 + col_step : 1 + col_step + tile_cols,
        ]

    height = neighbour(0, 0, 0)
    east = neighbour(1, 0, 0)
    north = neighbour(2, 0, 0)
    res_height = (
        tendency(height, angular)
        + neighbour(3, 0, 0)
        - neighbour(3, 0, -1)
        + neighbour(4, 0, 0)
        - neighbour(4, -1, 0)
    )
    north_mean = 0.25 * (north + neighbour(2, 0, 1) + neighbour(2, -1, 0) + neighbour(2, -1, 1))
    east_mean = 0.25 * (east + neighbour(1, 0, -1) + neighbour(1, 1, 0) + neighbour(1, 1, -1))
    res_east = (
        tendency(east, angular)
        + LINEAR_DRAG * east
        - rotation * north_mean
        + GRAVITY * (neighbour(0, 0, 1) - height)
    )
    res_north = (
        tendency(north, angular)
        + LINEAR_DRAG * north
        + rotation * east_mean
        + GRAVITY * (neighbour(0, 1, 0) - height)
    )
    return jnp.stack([res_height, res_east, res_north])


def friction_row(row_block, drag_row, table):
    highest = lax.Precision.HIGHEST
    series = jnp.einsum("tc,fcn->ftn", table, row_block, precision=highest)
    base_east, base_north, step_east, step_north = (series[0], series[1], series[2], series[3])
    magnitude = jnp.sqrt(base_east * base_east + base_north * base_north + SPEED_SOFT)
    projected = (base_east * step_east + base_north * step_north) / magnitude
    force_east = drag_row * (magnitude * step_east + base_east * projected)
    force_north = drag_row * (magnitude * step_north + base_north * projected)
    forces = jnp.stack([force_east, force_north])
    analysed = jnp.einsum("tc,ftn->fcn", table, forces, precision=highest) * (2.0 / table.shape[0])
    drag_rate = drag_row * jnp.mean(magnitude, axis=0)
    return (analysed, drag_rate)


def precondition(residual, angular, rotation, drag_rate):
    shaped = residual.reshape((3, residual.shape[1] // 2, 2) + residual.shape[2:])
    cos_part = shaped[:, :, 0]
    sin_part = shaped[:, :, 1]
    height_cos = -sin_part[0] / angular
    height_sin = cos_part[0] / angular
    real_rate = drag_rate + LINEAR_DRAG
    det_real = real_rate * real_rate - angular * angular + rotation * rotation
    det_imag = 2.0 * real_rate * angular
    det_norm = det_real * det_real + det_imag * det_imag
    inv_real = det_real / det_norm
    inv_imag = -det_imag / det_norm
    east_re = cos_part[1]
    east_im = -sin_part[1]
    north_re = cos_part[2]
    north_im = -sin_part[2]
    num_east_re = real_rate * east_re - angular * east_im + rotation * north_re
    num_east_im = real_rate * east_im + angular * east_re + rotation * north_im
    num_north_re = -rotation * east_re + real_rate * north_re - angular * north_im
    num_north_im = -rotation * east_im + real_rate * north_im + angular * north_re
    east_out_re = num_east_re * inv_real - num_east_im * inv_imag
    east_out_im = num_east_re * inv_imag + num_east_im * inv_real
    north_out_re = num_north_re * inv_real - num_north_im * inv_imag
    north_out_im = num_north_re * inv_imag + num_north_im * inv_real
    cosines = jnp.stack([height_cos, east_out_re, north_out_re])
    sines = jnp.stack([height_sin, -east_out_im, -north_out_im])
    return jnp.stack([cosines, sines], axis=2).reshape(residual.shape)


def friction_band(flows_band, drag_band, table):
    highest = lax.Precision.HIGHEST
    fields, coefs, rows, cols = flows_band.shape
    block = flows_band.reshape(fields, coefs, rows * cols)
    series = jnp.einsum("tc,fcn->ftn", table, block, precision=highest)
    base_east, base_north, step_east, step_north = (series[0], series[1], series[2], series[3])
    drag_row = drag_band.reshape(1, rows * cols)
    magnitude = jnp.sqrt(base_east * base_east + base_north * base_north + SPEED_SOFT)
    projected = (base_east * step_east + base_north * step_north) / magnitude
    force_east = drag_row * (magnitude * step_east + base_east * projected)
    force_north = drag_row * (magnitude * step_north + base_north * projected)
    forces = jnp.stack([force_east, force_north])
    analysed = jnp.einsum("tc,ftn->fcn", table, forces, precision=highest) * (2.0 / table.shape[0])
    drag_rate = drag_row[0] * lax.optimization_barrier(jnp.mean(magnitude, axis=0))
    return (analysed.reshape(2, coefs, rows, cols), drag_rate.reshape(rows, cols))


def local(direction, base_flow, water_depth, drag_factor, wet_mask):
    local_coefs = direction.shape[1]
    tile_rows = direction.shape[2]
    tile_cols = direction.shape[3]
    groups = lax.axis_size("freq")
    member = lax.axis_index("freq")
    band_rows = tile_rows // groups
    lat_place = lax.axis_index("lat")
    lat_count = lax.axis_size("lat")
    total_rows = tile_rows * lat_count
    wet_cells = wet_mask.astype(jnp.float32)
    height = direction[0] * wet_cells
    east = direction[1] * wet_cells
    north = direction[2] * wet_cells
    flows = jnp.concatenate([base_flow, jnp.stack([east, north])], axis=0)
    flows_band = lax.all_to_all(flows, "freq", split_axis=2, concat_axis=1, tiled=True)
    planes = jnp.stack([height, east, north, water_depth * east, water_depth * north])
    extended = extended_2(planes, (("lat", 2), ("lon", 3)), 1)
    rim_keep = jnp.ones((tile_rows + 2,), jnp.float32)
    rim_keep = rim_keep.at[0].set(jnp.where(lat_place == 0, 0.0, 1.0))
    rim_keep = rim_keep.at[tile_rows + 1].set(jnp.where(lat_place == lat_count - 1, 0.0, 1.0))
    extended = extended * rim_keep[:, None]
    local_count = local_coefs // 2
    first_con = member * local_count
    angular_local = OMEGA_STEP * (first_con + jnp.arange(local_count, dtype=jnp.int32) + 1).astype(
        jnp.float32
    )
    row_global = lat_place * tile_rows + jnp.arange(tile_rows, dtype=jnp.int32)
    rotation = rotation_of(row_global, total_rows)
    linear_part = linear_residual(
        extended, tile_rows, tile_cols, angular_local[:, None, None], rotation[:, None]
    )
    table = samples_table(NTIME, NCON)
    band_start = member * band_rows
    drag_band = lax.dynamic_slice_in_dim(drag_factor, band_start, band_rows, 0)
    analysed_band, drag_rate_band = friction_band(flows_band, drag_band, table)
    friction = lax.all_to_all(analysed_band, "freq", split_axis=1, concat_axis=2, tiled=True)
    drag_rate = lax.all_gather(drag_rate_band, "freq", axis=0, tiled=True)
    residual = (
        linear_part + jnp.concatenate([jnp.zeros_like(friction[:1]), friction], axis=0)
    ) * wet_cells
    return precondition(residual, angular_local[:, None, None], rotation[:, None], drag_rate)


def solution(mesh):
    placed = (
        P(None, "freq", "lat", "lon"),
        P(None, "freq", "lat", "lon"),
        P("lat", "lon"),
        P("lat", "lon"),
        P("lat", "lon"),
    )
    return jax.shard_map(
        local, mesh=mesh, in_specs=placed, out_specs=P(None, "freq", "lat", "lon"), check_vma=False
    )
```

profile of v0, /device:TPU:2, one launch (start us, length us, event | category | flops | bytes accessed | tf_op | source)
XLA Modules:
  0.0 294.2 jit_solution(5827438192637905519)
XLA Ops:
  1.0 2.4 multiply_dynamic-update-slice_fusion.2
  3.4 2.5 constant_dynamic-update-slice_fusion.1
  5.9 2.7 constant_dynamic-update-slice_fusion
  9.9 1.4 copy.87
  11.3 2.7 pad_maximum_fusion
  13.9 9.2 %all-to-all-start = ((f32[4,4,128,512]{3,1,0,2:T(4,128)}), f32[4,4,128,512]{3,1,0,2:T(4,128)}, u32[]{:S(2)}, u32[]{:S(2)}) async-start(f32[4,4,128,512]{3,1,0,2:T(4,128)} %pad_maximum_fusion), calls=%async_computation | async-start | bytes 8388608 | tf_op jit(solution)/shard_map/all_to_all | solution.py:160
  23.4 1.2 multiply_dynamic-update-slice_fusion.1
  25.8 93.7 %all-to-all-done = f32[4,4,128,512]{3,1,0,2:T(4,128)} async-done(((f32[4,4,128,512]{3,1,0,2:T(4,128)}), f32[4,4,128,512]{3,1,0,2:T(4,128)}, u32[]{:S(2)}, u32[]{:S(2)}) %all-to-all-start) | async-done | bytes 4194336 | tf_op jit(solution)/shard_map/all_to_all | solution.py:160
  119.4 6.6 %copy.110 = f32[4,4,8,16,512]{4,3,1,2,0:T(8,128)} copy(f32[4,4,8,16,512]{4,1,0,3,2:T(4,128)} %bitcast.8) | data formatting | bytes 8388608 | tf_op jit(solution)/shard_map/all_to_all | solution.py:160
  126.1 5.0 %reshape.520 = f32[4,32,8192]{2,1,0:T(8,128)} reshape(f32[4,8,4,16,512]{4,3,2,1,0:T(8,128)} %bitcast.142) | data formatting | bytes 8388608 | tf_op jit(solution)/shard_map/reshape | solution.py:131
  131.1 47.7 %convolution_bitcast_fusion = f32[4,256,8192]{2,1,0:T(8,128)} fusion(f32[4,32,8192]{2,1,0:T(8,128)} %reshape.520, f32[256,32,1]{0,1,2:T(8,128)S(1)} %reshape.526), kind=kOutput, calls=%fused_computation | convolution fusion | flops 3221225472 | bytes 37781504 | tf_op jit(solution)/shard_map/tc,fcn->ftn/dot_general | solution.py:132
  178.8 18.2 %add_multiply_fusion.1 = (f32[1,256,8192]{2,1,0:T(8,128)}, f32[1,256,8192]{2,1,0:T(8,128)}, f32[8192]{0:T(1024)S(1)}) fusion(f32[4,256,8192]{2,1,0:T(8,128)} %convolution_bitcast_fusion, f32[8192]{0:T(1024)S(1)} %bitcast.154), kind=kLoop, calls=%fused_computation.7 | loop fusion | flops 35643392 | bytes 50397184 | tf_op jit(solution)/shard_map/mul | solution.py:137
  197.0 13.7 %fusion.4 = f32[2,8192,32]{1,2,0:T(8,128)S(1)} fusion(f32[256,32,1]{0,1,2:T(8,128)S(1)} %reshape.526, f32[1,256,8192]{2,1,0:T(8,128)} %get-tuple-element.40, f32[1,256,8192]{2,1,0:T(8,128)} %get-tuple-element.39), kind=kOutput, calls=%fused_computation.5 | convolution fusion | flops 1615331328 | bytes 18907136 | tf_op jit(solution)/shard_map/tc,ftn->fcn/dot_general | solution.py:140
  210.7 1.2 copy.108
  211.9 1.6 copy.92
  213.5 3.6 %all-to-all-start.1 = ((f32[2,32,16,512]{3,2,0,1:T(8,128)}), f32[2,32,16,512]{3,2,0,1:T(8,128)S(1)}, u32[]{:S(2)}, u32[]{:S(2)}) async-start(f32[2,32,16,512]{3,2,0,1:T(8,128)} %copy.92), calls=%async_computation.1 | async-start | bytes 4194304 | tf_op jit(solution)/shard_map/all_to_all | solution.py:181
  218.3 3.3 %collective-permute-start = (f32[5,4,1,512]{3,2,1,0:T(1,128)S(1)}, f32[5,4,1,512]{3,2,1,0:T(1,128)S(1)}, u32[]{:S(2)}, u32[]{:S(2)}) collective-permute-start(f32[5,4,1,512]{3,2,1,0:T(1,128)S(1)} %get-tuple-element.49), channel_id=1, source_target_pairs={{0,4},{4,8},{8,12},{12,16},{16,20},{20,24},{24,28},{28,0},{1,5},{5... | collective-permute-start | bytes 122888 | tf_op jit(solution)/shard_map/ppermute | solution.py:21
  221.5 1.4 collective-permute-start.1
  223.0 1.7 collective-permute-done
  224.7 2.5 collective-permute-done.1
  227.2 3.8 %pad_maximum_fusion.4 = (f32[5,4,130,1]{3,2,1,0:T(8,128)}, f32[5,4,130,1]{3,2,1,0:T(8,128)}) fusion(f32[5,4,1,512]{3,2,1,0:T(1,128)S(1)} %collective-permute-done.1, f32[5,4,128,512]{3,2,1,0:T(8,128)} %multiply_dynamic-update-slice_fusion, f32[5,4,1,512]{3,2,1,0:T(1,128)S(1)} %collective-permute-done), kind=kLoop, calls=%fused_computation.22 | loop fusion | flops 10400 | bytes 5345600 | tf_op jit(solution)/shard_map/slice | solution.py:22
  231.0 2.5 copy.83
  233.6 2.6 copy.84
  236.2 1.8 collective-permute-start.3
  238.0 1.6 copy.85
  239.6 1.6 copy.86
  241.2 6.2 %maximum_multiply_fusion = f32[5,4,130,514]{3,2,1,0:T(8,128)S(1)} fusion(f32[5,4,130,1]{3,2,1,0:T(8,128)} %copy.86, f32[5,4,1,512]{3,2,1,0:T(1,128)S(1)} %collective-permute-done.1, f32[5,4,128,512]{3,2,1,0:T(8,128)} %multiply_dynamic-update-slice_fusion, f32[5,4,1,512]{3,2,1,0:T(1,128)S(1)} %collective-permute-done, f32[5,4,130,1]{3,2,1,0:T(8,128)} %copy.85, ...), kind=kLoop, calls=%fused_computation.12 | loop fusion | flops 6682000 | bytes 10691720 | tf_op jit(solution)/shard_map/mul | solution.py:166
  248.1 2.7 slice_subtract_fusion.2
  251.4 3.9 %fusion.12 = (f32[1,4,128,512]{3,2,1,0:T(8,128)}, f32[1,4,128,512]{3,2,1,0:T(8,128)}) fusion(f32[5,4,130,514]{3,2,1,0:T(8,128)S(1)} %maximum_multiply_fusion, f32[128]{0:T(128)S(1)} %broadcast_multiply_fusion.2, f32[1,4,128,512]{3,2,1,0:T(8,128)S(1)} %bitcast.151, f32[1,4,128,512]{3,2,1,0:T(8,128)S(1)} %bitcast.150), kind=kLoop, calls=%fused_computation.31 | loop fusion | flops 4718592 | bytes 15729152 | tf_op jit(solution)/shard_map/add | solution.py:71
  255.3 31.2 %all_gather.3 = f32[128,512]{1,0:T(8,128)S(1)} all-gather(f32[16,512]{1,0:T(8,128)S(1)} %reshape.524), channel_id=1, replica_groups=mesh['freq'=8,'lat'=8,'lon'=4] {'freq'}, dimensions={0}, use_global_device_ids=true | all-gather | bytes 294912 | tf_op jit(solution)/shard_map/all_gather | solution.py:182
  288.2 1.9 fusion.8
  291.9 2.0 copy.100
  (51 shorter events, 9.6 us)
Async XLA Ops:
  0.0 23.4 %copy-start = (f32[128,512]{1,0:T(8,128)S(1)}, f32[128,512]{1,0:T(8,128)}, u32[]{:S(2)}) copy-start(f32[128,512]{1,0:T(8,128)} %param.12) | copy-start | bytes 786436
  5.9 4.0 %copy-start.4 = (f32[2,4,128,512]{3,2,1,0:T(8,128)S(1)}, f32[2,4,128,512]{3,2,1,0:T(8,128)}, u32[]{:S(2)}) copy-start(f32[2,4,128,512]{3,2,1,0:T(8,128)} %param.10) | copy-start | bytes 6291460
  13.9 9.5 %copy-start.5 = (f32[128,512]{1,0:T(8,128)S(1)}, f32[128,512]{1,0:T(8,128)}, u32[]{:S(2)}) copy-start(f32[128,512]{1,0:T(8,128)} %param.11) | copy-start | bytes 786436
  13.9 105.5 %all-to-all-start = ((f32[4,4,128,512]{3,1,0,2:T(4,128)}), f32[4,4,128,512]{3,1,0,2:T(4,128)}, u32[]{:S(2)}, u32[]{:S(2)}) async-start(f32[4,4,128,512]{3,1,0,2:T(4,128)} %pad_maximum_fusion), calls=%async_computation | async-start | bytes 8388608 | tf_op jit(solution)/shard_map/all_to_all | solution.py:160
  213.5 73.1 %all-to-all-start.1 = ((f32[2,32,16,512]{3,2,0,1:T(8,128)}), f32[2,32,16,512]{3,2,0,1:T(8,128)S(1)}, u32[]{:S(2)}, u32[]{:S(2)}) async-start(f32[2,32,16,512]{3,2,0,1:T(8,128)} %copy.92), calls=%async_computation.1 | async-start | bytes 4194304 | tf_op jit(solution)/shard_map/all_to_all | solution.py:181
  218.3 6.5 %collective-permute-start = (f32[5,4,1,512]{3,2,1,0:T(1,128)S(1)}, f32[5,4,1,512]{3,2,1,0:T(1,128)S(1)}, u32[]{:S(2)}, u32[]{:S(2)}) collective-permute-start(f32[5,4,1,512]{3,2,1,0:T(1,128)S(1)} %get-tuple-element.49), channel_id=1, source_target_pairs={{0,4},{4,8},{8,12},{12,16},{16,20},{20,24},{24,28},{28,0},{1,5},{5... | collective-permute-start | bytes 122888 | tf_op jit(solution)/shard_map/ppermute | solution.py:21
  221.5 5.7 %collective-permute-start.1 = (f32[5,4,1,512]{3,2,1,0:T(1,128)S(1)}, f32[5,4,1,512]{3,2,1,0:T(1,128)S(1)}, u32[]{:S(2)}, u32[]{:S(2)}) collective-permute-start(f32[5,4,1,512]{3,2,1,0:T(1,128)S(1)} %get-tuple-element.50), channel_id=1, source_target_pairs={{4,0},{8,4},{12,8},{16,12},{20,16},{24,20},{28,24},{0,28},{5,1},{9... | collective-permute-start | bytes 122888 | tf_op jit(solution)/shard_map/ppermute | solution.py:24
  233.5 4.4 %collective-permute-start.2 = (f32[5,4,130,1]{2,0,3,1:T(8,128)S(1)}, f32[5,4,130,1]{2,0,3,1:T(8,128)S(1)}, u32[]{:S(2)}, u32[]{:S(2)}) collective-permute-start(f32[5,4,130,1]{2,0,3,1:T(8,128)S(1)} %copy.83), channel_id=1, source_target_pairs={{0,1},{1,2},{2,3},{3,0},{4,5},{5,6},{6,7},{7,4},{8,9},{9,10},{10,1... | collective-permute-start | bytes 31208 | tf_op jit(solution)/shard_map/ppermute | solution.py:21
  236.2 3.4 %collective-permute-start.3 = (f32[5,4,130,1]{2,0,3,1:T(8,128)S(1)}, f32[5,4,130,1]{2,0,3,1:T(8,128)S(1)}, u32[]{:S(2)}, u32[]{:S(2)}) collective-permute-start(f32[5,4,130,1]{2,0,3,1:T(8,128)S(1)} %copy.84), channel_id=1, source_target_pairs={{1,0},{2,1},{3,2},{0,3},{5,4},{6,5},{7,6},{4,7},{9,8},{10,9},{11,1... | collective-permute-start | bytes 31208 | tf_op jit(solution)/shard_map/ppermute | solution.py:24
  286.6 1.2 copy-start.2
  286.7 1.5 copy-start.3
  291.6 2.3 copy-start.1
where the time goes:
time: 298 us; the launch traced here: 294 us
  waiting for transfers between devices  97.9 us (33%)
  matrix products  61.4 us (21%)
  other arithmetic  53.1 us (18%)
  blocking collectives  31.2 us (10%)
  local copies, waits for them, and re-layouts  30.6 us (10%)
  starting transfers between devices  19.3 us (6%)
    all_to_all x1, waiting for transfers between devices, local(): lax.all_to_all(flows, 'freq', split_axis=2, concat_axis=1, tiled=True)  93.7 us
    dot_general x1, matrix products, friction_band(): series = jnp.einsum('tc,fcn->ftn', table, block, precision=highest)  47.7 us
    all_gather x1, blocking collectives, local(): drag_rate = lax.all_gather(drag_rate_band, 'freq', axis=0, tiled=True)  31.2 us
    mul x1, other arithmetic, friction_band(): force_east = drag_row * (magnitude * step_east + base_east * projected)  18.2 us
    dot_general x1, matrix products, friction_band(): jnp.einsum('tc,ftn->fcn', table, forces, precision=highest)  13.7 us
    all_to_all x1, starting transfers between devices, local(): lax.all_to_all(flows, 'freq', split_axis=2, concat_axis=1, tiled=True)  9.18 us
    unnamed x4, other arithmetic  8.68 us
    all_to_all x1, local copies, waits for them, and re-layouts, local(): lax.all_to_all(flows, 'freq', split_axis=2, concat_axis=1, tiled=True)  6.64 us
  transfers between devices with their start and end apart: 6, of which 3 were waited for; matrix products, arithmetic and copies ran while one was open for 10% of the time, Pallas kernels for 0%

commit v1 on v0

--- a/solution.py
+++ b/solution.py
@@ -179,7 +179,12 @@
     drag_band = lax.dynamic_slice_in_dim(drag_factor, band_start, band_rows, 0)
     analysed_band, drag_rate_band = friction_band(flows_band, drag_band, table)
     friction = lax.all_to_all(analysed_band, "freq", split_axis=1, concat_axis=2, tiled=True)
-    drag_rate = lax.all_gather(drag_rate_band, "freq", axis=0, tiled=True)
+    drag_rate = jnp.concatenate(
+        lax.all_to_all(
+            jnp.stack([drag_rate_band for _ in range(lax.axis_size("freq"))]), "freq", 0, 0
+        ),
+        axis=0,
+    )
     residual = (
         linear_part + jnp.concatenate([jnp.zeros_like(friction[:1]), friction], axis=0)
     ) * wet_cells

time: 298 us -> 287 us (0.963)
  blocking collectives: 31.2 us -> 0 us
  waiting for transfers between devices: 97.9 us -> 111 us
  starting transfers between devices: 19.3 us -> 26.2 us
    all_gather x1 -> x0, blocking collectives: 31.2 us -> none  [local(): drag_rate = lax.all_gather(drag_rate_band, 'freq', axis=0, tiled=True)]
    all_to_all x1, waiting for transfers between devices: 0.01 us -> 12.8 us  [local(): lax.all_to_all(analysed_band, 'freq', split_axis=1, concat_axis=2, tiled=...]
    all_to_all x1, starting transfers between devices: 3.6 us -> 7.12 us  [local(): lax.all_to_all(analysed_band, 'freq', split_axis=1, concat_axis=2, tiled=...]
    all_to_all x0 -> x1, starting transfers between devices: none -> 3.41 us  [local(): lax.all_to_all(jnp.stack([drag_rate_band for _ in range(lax.axis_size('fr...]
  transfers between devices with their start and end apart: 6 -> 7, of which waited for: 3 -> 4; matrix products, arithmetic and copies ran while one was open for 10% -> 16% of each run, Pallas kernels for 0% -> 0%
where the time goes in v1:
time: 287 us; the launch traced here: 283 us
  waiting for transfers between devices  111 us (39%)
  matrix products  61.4 us (21%)
  other arithmetic  53 us (18%)
  local copies, waits for them, and re-layouts  31.3 us (11%)
  starting transfers between devices  26.2 us (9%)
    all_to_all x1, waiting for transfers between devices, local(): lax.all_to_all(flows, 'freq', split_axis=2, concat_axis=1, tiled=True)  93.7 us
    dot_general x1, matrix products, friction_band(): series = jnp.einsum('tc,fcn->ftn', table, block, precision=highest)  47.7 us
    mul x1, other arithmetic, friction_band(): force_east = drag_row * (magnitude * step_east + base_east * projected)  18.2 us
    dot_general x1, matrix products, friction_band(): jnp.einsum('tc,ftn->fcn', table, forces, precision=highest)  13.7 us
    all_to_all x1, waiting for transfers between devices, local(): lax.all_to_all(analysed_band, 'freq', split_axis=1, concat_axis=2, tiled=...  12.8 us
    all_to_all x1, starting transfers between devices, local(): lax.all_to_all(flows, 'freq', split_axis=2, concat_axis=1, tiled=True)  9.12 us
    unnamed x4, other arithmetic  8.66 us
    all_to_all x1, starting transfers between devices, local(): lax.all_to_all(analysed_band, 'freq', split_axis=1, concat_axis=2, tiled=...  7.12 us
  transfers between devices with their start and end apart: 7, of which 4 were waited for; matrix products, arithmetic and copies ran while one was open for 16% of the time, Pallas kernels for 0%

profile of v1, /device:TPU:2, one launch (start us, length us, event | category | flops | bytes accessed | tf_op | source)
XLA Modules:
  0.0 283.3 jit_solution(1385850749049875702)
XLA Ops:
  1.0 2.3 multiply_dynamic-update-slice_fusion.2
  3.4 2.5 constant_dynamic-update-slice_fusion.1
  5.9 2.6 constant_dynamic-update-slice_fusion
  9.9 1.4 copy.87
  11.3 2.7 pad_maximum_fusion
  13.9 9.1 %all-to-all-start = ((f32[4,4,128,512]{3,1,0,2:T(4,128)}), f32[4,4,128,512]{3,1,0,2:T(4,128)}, u32[]{:S(2)}, u32[]{:S(2)}) async-start(f32[4,4,128,512]{3,1,0,2:T(4,128)} %pad_maximum_fusion), calls=%async_computation | async-start | bytes 8388608 | tf_op jit(solution)/shard_map/all_to_all | solution.py:160
  25.7 93.7 %all-to-all-done = f32[4,4,128,512]{3,1,0,2:T(4,128)} async-done(((f32[4,4,128,512]{3,1,0,2:T(4,128)}), f32[4,4,128,512]{3,1,0,2:T(4,128)}, u32[]{:S(2)}, u32[]{:S(2)}) %all-to-all-start) | async-done | bytes 4194336 | tf_op jit(solution)/shard_map/all_to_all | solution.py:160
  119.4 6.6 %copy.110 = f32[4,4,8,16,512]{4,3,1,2,0:T(8,128)} copy(f32[4,4,8,16,512]{4,1,0,3,2:T(4,128)} %bitcast.8) | data formatting | bytes 8388608 | tf_op jit(solution)/shard_map/all_to_all | solution.py:160
  126.0 5.0 %reshape.532 = f32[4,32,8192]{2,1,0:T(8,128)} reshape(f32[4,8,4,16,512]{4,3,2,1,0:T(8,128)} %bitcast.145) | data formatting | bytes 8388608 | tf_op jit(solution)/shard_map/reshape | solution.py:131
  131.0 47.7 %convolution_bitcast_fusion = f32[4,256,8192]{2,1,0:T(8,128)} fusion(f32[4,32,8192]{2,1,0:T(8,128)} %reshape.532, f32[256,32,1]{0,1,2:T(8,128)S(1)} %reshape.537), kind=kOutput, calls=%fused_computation | convolution fusion | flops 3221225472 | bytes 37781504 | tf_op jit(solution)/shard_map/tc,fcn->ftn/dot_general | solution.py:132
  178.7 18.2 %add_multiply_fusion.1 = (f32[1,256,8192]{2,1,0:T(8,128)}, f32[1,256,8192]{2,1,0:T(8,128)}, f32[8192]{0:T(1024)S(1)}) fusion(f32[4,256,8192]{2,1,0:T(8,128)} %convolution_bitcast_fusion, f32[8192]{0:T(1024)S(1)} %bitcast.158), kind=kLoop, calls=%fused_computation.7 | loop fusion | flops 35643392 | bytes 50397184 | tf_op jit(solution)/shard_map/mul | solution.py:137
  197.7 3.4 %all-to-all-start.2 = ((f32[8,16,512]{2,1,0:T(8,128)}), f32[8,16,512]{2,1,0:T(8,128)S(1)}, u32[]{:S(2)}, u32[]{:S(2)}) async-start(f32[8,16,512]{2,1,0:T(8,128)} %stack.33), calls=%async_computation.2 | async-start | bytes 524288 | tf_op jit(solution)/shard_map/all_to_all | solution.py:183
  201.1 13.7 %fusion.4 = f32[2,8192,32]{1,2,0:T(8,128)S(1)} fusion(f32[256,32,1]{0,1,2:T(8,128)S(1)} %reshape.537, f32[1,256,8192]{2,1,0:T(8,128)} %get-tuple-element.40, f32[1,256,8192]{2,1,0:T(8,128)} %get-tuple-element.39), kind=kOutput, calls=%fused_computation.5 | convolution fusion | flops 1615331328 | bytes 18907136 | tf_op jit(solution)/shard_map/tc,ftn->fcn/dot_general | solution.py:140
  214.8 1.2 copy.108
  216.0 1.6 copy.92
  217.6 7.1 %all-to-all-start.1 = ((f32[2,32,16,512]{3,2,0,1:T(8,128)}), f32[2,32,16,512]{3,2,0,1:T(8,128)S(1)}, u32[]{:S(2)}, u32[]{:S(2)}) async-start(f32[2,32,16,512]{3,2,0,1:T(8,128)} %copy.92), calls=%async_computation.1 | async-start | bytes 4194304 | tf_op jit(solution)/shard_map/all_to_all | solution.py:181
  225.9 3.3 %collective-permute-start = (f32[5,4,1,512]{3,2,1,0:T(1,128)S(1)}, f32[5,4,1,512]{3,2,1,0:T(1,128)S(1)}, u32[]{:S(2)}, u32[]{:S(2)}) collective-permute-start(f32[5,4,1,512]{3,2,1,0:T(1,128)S(1)} %get-tuple-element.49), channel_id=1, source_target_pairs={{0,4},{4,8},{8,12},{12,16},{16,20},{20,24},{24,28},{28,0},{1,5},{5... | collective-permute-start | bytes 122888 | tf_op jit(solution)/shard_map/ppermute | solution.py:21
  229.1 1.4 collective-permute-start.1
  230.6 1.7 collective-permute-done
  232.3 2.5 collective-permute-done.1
  234.8 3.8 %pad_maximum_fusion.4 = (f32[5,4,130,1]{3,2,1,0:T(8,128)}, f32[5,4,130,1]{3,2,1,0:T(8,128)}) fusion(f32[5,4,1,512]{3,2,1,0:T(1,128)S(1)} %collective-permute-done.1, f32[5,4,128,512]{3,2,1,0:T(8,128)} %multiply_dynamic-update-slice_fusion, f32[5,4,1,512]{3,2,1,0:T(1,128)S(1)} %collective-permute-done), kind=kLoop, calls=%fused_computation.22 | loop fusion | flops 10400 | bytes 5345600 | tf_op jit(solution)/shard_map/slice | solution.py:22
  238.6 2.5 copy.83
  241.2 2.6 copy.84
  243.8 1.8 collective-permute-start.3
  245.6 1.6 copy.85
  247.2 1.6 copy.86
  248.8 6.2 %maximum_multiply_fusion = f32[5,4,130,514]{3,2,1,0:T(8,128)S(1)} fusion(f32[5,4,130,1]{3,2,1,0:T(8,128)} %copy.86, f32[5,4,1,512]{3,2,1,0:T(1,128)S(1)} %collective-permute-done.1, f32[5,4,128,512]{3,2,1,0:T(8,128)} %multiply_dynamic-update-slice_fusion, f32[5,4,1,512]{3,2,1,0:T(1,128)S(1)} %collective-permute-done, f32[5,4,130,1]{3,2,1,0:T(8,128)} %copy.85, ...), kind=kLoop, calls=%fused_computation.12 | loop fusion | flops 6682000 | bytes 10691720 | tf_op jit(solution)/shard_map/mul | solution.py:166
  255.8 2.7 slice_subtract_fusion.2
  259.0 3.9 %fusion.12 = (f32[1,4,128,512]{3,2,1,0:T(8,128)}, f32[1,4,128,512]{3,2,1,0:T(8,128)}) fusion(f32[5,4,130,514]{3,2,1,0:T(8,128)S(1)} %maximum_multiply_fusion, f32[128]{0:T(128)S(1)} %broadcast_multiply_fusion.2, f32[1,4,128,512]{3,2,1,0:T(8,128)S(1)} %bitcast.154, f32[1,4,128,512]{3,2,1,0:T(8,128)S(1)} %bitcast.153), kind=kLoop, calls=%fused_computation.31 | loop fusion | flops 4718592 | bytes 15729152 | tf_op jit(solution)/shard_map/add | solution.py:71
  263.0 12.8 %all-to-all-done.1 = f32[2,32,16,512]{3,2,0,1:T(8,128)S(1)} async-done(((f32[2,32,16,512]{3,2,0,1:T(8,128)}), f32[2,32,16,512]{3,2,0,1:T(8,128)S(1)}, u32[]{:S(2)}, u32[]{:S(2)}) %all-to-all-start.1) | async-done | bytes 2097184 | tf_op jit(solution)/shard_map/all_to_all | solution.py:181
  277.4 1.9 fusion.8
  281.1 2.0 copy.100
  (54 shorter events, 11.5 us)
Async XLA Ops:
  0.0 23.3 %copy-start = (f32[128,512]{1,0:T(8,128)S(1)}, f32[128,512]{1,0:T(8,128)}, u32[]{:S(2)}) copy-start(f32[128,512]{1,0:T(8,128)} %param.12) | copy-start | bytes 786436
  5.9 4.0 %copy-start.4 = (f32[2,4,128,512]{3,2,1,0:T(8,128)S(1)}, f32[2,4,128,512]{3,2,1,0:T(8,128)}, u32[]{:S(2)}) copy-start(f32[2,4,128,512]{3,2,1,0:T(8,128)} %param.10) | copy-start | bytes 6291460
  13.9 9.4 %copy-start.5 = (f32[128,512]{1,0:T(8,128)S(1)}, f32[128,512]{1,0:T(8,128)}, u32[]{:S(2)}) copy-start(f32[128,512]{1,0:T(8,128)} %param.11) | copy-start | bytes 786436
  13.9 105.4 %all-to-all-start = ((f32[4,4,128,512]{3,1,0,2:T(4,128)}), f32[4,4,128,512]{3,1,0,2:T(4,128)}, u32[]{:S(2)}, u32[]{:S(2)}) async-start(f32[4,4,128,512]{3,1,0,2:T(4,128)} %pad_maximum_fusion), calls=%async_computation | async-start | bytes 8388608 | tf_op jit(solution)/shard_map/all_to_all | solution.py:160
  197.7 19.9 %all-to-all-start.2 = ((f32[8,16,512]{2,1,0:T(8,128)}), f32[8,16,512]{2,1,0:T(8,128)S(1)}, u32[]{:S(2)}, u32[]{:S(2)}) async-start(f32[8,16,512]{2,1,0:T(8,128)} %stack.33), calls=%async_computation.2 | async-start | bytes 524288 | tf_op jit(solution)/shard_map/all_to_all | solution.py:183
  217.6 58.2 %all-to-all-start.1 = ((f32[2,32,16,512]{3,2,0,1:T(8,128)}), f32[2,32,16,512]{3,2,0,1:T(8,128)S(1)}, u32[]{:S(2)}, u32[]{:S(2)}) async-start(f32[2,32,16,512]{3,2,0,1:T(8,128)} %copy.92), calls=%async_computation.1 | async-start | bytes 4194304 | tf_op jit(solution)/shard_map/all_to_all | solution.py:181
  225.9 6.5 %collective-permute-start = (f32[5,4,1,512]{3,2,1,0:T(1,128)S(1)}, f32[5,4,1,512]{3,2,1,0:T(1,128)S(1)}, u32[]{:S(2)}, u32[]{:S(2)}) collective-permute-start(f32[5,4,1,512]{3,2,1,0:T(1,128)S(1)} %get-tuple-element.49), channel_id=1, source_target_pairs={{0,4},{4,8},{8,12},{12,16},{16,20},{20,24},{24,28},{28,0},{1,5},{5... | collective-permute-start | bytes 122888 | tf_op jit(solution)/shard_map/ppermute | solution.py:21
  229.1 5.7 %collective-permute-start.1 = (f32[5,4,1,512]{3,2,1,0:T(1,128)S(1)}, f32[5,4,1,512]{3,2,1,0:T(1,128)S(1)}, u32[]{:S(2)}, u32[]{:S(2)}) collective-permute-start(f32[5,4,1,512]{3,2,1,0:T(1,128)S(1)} %get-tuple-element.50), channel_id=1, source_target_pairs={{4,0},{8,4},{12,8},{16,12},{20,16},{24,20},{28,24},{0,28},{5,1},{9... | collective-permute-start | bytes 122888 | tf_op jit(solution)/shard_map/ppermute | solution.py:24
  241.2 4.4 %collective-permute-start.2 = (f32[5,4,130,1]{2,0,3,1:T(8,128)S(1)}, f32[5,4,130,1]{2,0,3,1:T(8,128)S(1)}, u32[]{:S(2)}, u32[]{:S(2)}) collective-permute-start(f32[5,4,130,1]{2,0,3,1:T(8,128)S(1)} %copy.83), channel_id=1, source_target_pairs={{0,1},{1,2},{2,3},{3,0},{4,5},{5,6},{6,7},{7,4},{8,9},{9,10},{10,1... | collective-permute-start | bytes 31208 | tf_op jit(solution)/shard_map/ppermute | solution.py:21
  243.8 3.4 %collective-permute-start.3 = (f32[5,4,130,1]{2,0,3,1:T(8,128)S(1)}, f32[5,4,130,1]{2,0,3,1:T(8,128)S(1)}, u32[]{:S(2)}, u32[]{:S(2)}) collective-permute-start(f32[5,4,130,1]{2,0,3,1:T(8,128)S(1)} %copy.84), channel_id=1, source_target_pairs={{1,0},{2,1},{3,2},{0,3},{5,4},{6,5},{7,6},{4,7},{9,8},{10,9},{11,1... | collective-permute-start | bytes 31208 | tf_op jit(solution)/shard_map/ppermute | solution.py:24
  275.8 1.2 copy-start.2
  275.8 1.5 copy-start.3
  280.8 2.3 copy-start.1
